TPU v7x, 32 devices: a whole 2x2x4 slice. The times are simulated.
32 devices in a mesh: wide: 8 (over z, x), narrow: 4 (over y, core).
Axes of the slice: x: 2, y: 2, z: 4, core: 2. Of those that a mesh axis runs over, the one named last changes fastest.
Arguments:
- tokens: bfloat16 [16, 1024, 768], P('wide', 'narrow'), may hold values from -6 to 6
- segment_ids: int32 [16, 1024], P('wide'), may hold values from -1 to 7, as said below
- cotangent: bfloat16 [16, 1024, 768], P('wide', 'narrow'), may hold values from -6 to 6
- attn_w: float32 [4, 768, 768], P(None, 'wide', 'narrow')
- attn_m: float32 [4, 768, 768], P(None, 'wide', 'narrow')
- attn_v: float32 [4, 768, 768], P(None, 'wide', 'narrow')
- mlp_w: float32 [2, 768, 3072], P(None, 'wide', 'narrow')
- mlp_m: float32 [2, 768, 3072], P(None, 'wide', 'narrow')
- mlp_v: float32 [2, 768, 3072], P(None, 'wide', 'narrow')
- vectors: float32 [12, 768], replicated
- vec_m: float32 [12, 768], replicated
- vec_v: float32 [12, 768], replicated
Outputs:
- block_out: bfloat16 [16, 1024, 768], P('wide', 'narrow')
- block_input_gradient: float32 [16, 1024, 768], P('wide', 'narrow')
- attn_grad: float32 [4, 768, 768], P(None, 'wide', 'narrow')
- attn_new: float32 [4, 768, 768], P(None, 'wide', 'narrow')
- attn_m_new: float32 [4, 768, 768], P(None, 'wide', 'narrow')
- attn_v_new: float32 [4, 768, 768], P(None, 'wide', 'narrow')
- mlp_grad: float32 [2, 768, 3072], P(None, 'wide', 'narrow')
- mlp_new: float32 [2, 768, 3072], P(None, 'wide', 'narrow')
- mlp_m_new: float32 [2, 768, 3072], P(None, 'wide', 'narrow')
- mlp_v_new: float32 [2, 768, 3072], P(None, 'wide', 'narrow')
- vec_grad: float32 [12, 768], replicated
- vec_new: float32 [12, 768], replicated
- vec_m_new: float32 [12, 768], replicated
- vec_v_new: float32 [12, 768], replicated
Inputs may be any that keep to these rules, and one draw needn't show every extreme that they name: `segment_ids`: in each row the ids start at 0, never fall along the slots and are at most 7; the last slots of a row (at most 51) hold -1 for padding.
All inputs are finite; a program needn't handle non-finite values.
Results may differ from a plain program's by a relative error of at most 0.019.
Values may be sent and summed in bfloat16 or wider, within the bound.
No kernel may reach another device: no remote copies, remote signals or barrier semaphores. Data moves between devices by JAX's collectives and lax.ppermute only.
A program may use at most 128 MiB of HBM per device.

v0:
```python
import jax
import jax.numpy as jnp
from jax import lax
from jax.sharding import PartitionSpec as P

HEAD_DIM = 64
STEP = 10
EPS_NORM = 1e-06
MASKED_SCORE = -1e30
BETA_ONE = 0.5
BETA_TWO = 0.5
EPS_ADAM = 1e-08
RATE_MATRIX = 0.04
RATE_VECTOR = 0.3
DECAY_MATRIX = 0.05


def norm_shard_pieces(values_in, gain_vec, shift_vec):
    row_mean = jnp.mean(values_in, axis=-1, keepdims=True)
    centred = values_in - row_mean
    row_var = jnp.mean(centred * centred, axis=-1, keepdims=True)
    inv_std = lax.rsqrt(row_var + EPS_NORM)
    normed = centred * inv_std
    return (normed * gain_vec + shift_vec, normed, inv_std)


def norm_backward_pass(grad_out, normed, inv_std, gain_vec):
    scaled = grad_out * gain_vec
    return inv_std * (
        scaled
        - jnp.mean(scaled, axis=-1, keepdims=True)
        - normed * jnp.mean(scaled * normed, axis=-1, keepdims=True)
    )


def exact_gelu(values_in):
    return jax.nn.gelu(values_in, approximate=False)


def local_shard_portion(rows_in, sequence_count, start, count):
    shaped = rows_in.reshape(sequence_count, -1, rows_in.shape[-1])
    return lax.dynamic_slice_in_dim(shaped, start, count, 1)


def adamw_update(weight, first_mom, second, gradient, step_rate, decay_rate):
    first_new = BETA_ONE * first_mom + (1.0 - BETA_ONE) * gradient
    second_new = BETA_TWO * second + (1.0 - BETA_TWO) * gradient * gradient
    corrected = (
        first_new
        / (1.0 - BETA_ONE**STEP)
        / (jnp.sqrt(second_new / (1.0 - BETA_TWO**STEP)) + EPS_ADAM)
    )
    return (weight - step_rate * (corrected + decay_rate * weight), first_new, second_new)


def local(
    tokens,
    segment_ids,
    cotangent,
    attn_w,
    attn_m,
    attn_v,
    mlp_w,
    mlp_m,
    mlp_v,
    vectors,
    vec_m,
    vec_v,
):
    narrow_count = lax.axis_size("narrow")
    narrow_index = lax.axis_index("narrow")
    sequence_count, shard_length, width = tokens.shape
    seq_len = segment_ids.shape[1]
    token_count = sequence_count * seq_len
    local_cols = attn_w.shape[2]
    local_hidden = mlp_w.shape[2]
    head_local = local_cols // HEAD_DIM
    block_len = min(seq_len, 512)
    block_count = seq_len // block_len
    scale = HEAD_DIM ** (-0.5)
    shard_offset = narrow_index * shard_length
    attn_full, mlp_full = (
        lax.all_gather(attn_w.astype(jnp.bfloat16), "wide", axis=1, tiled=True),
        lax.all_gather(mlp_w.astype(jnp.bfloat16), "wide", axis=1, tiled=True),
    )
    tokens_all, cot_all = (
        lax.all_gather(tokens, "narrow", axis=1, tiled=True),
        lax.all_gather(cotangent, "narrow", axis=1, tiled=True),
    )
    input_tokens = tokens_all.reshape(token_count, width).astype(jnp.float32)
    cotangent_token_rows = cot_all.reshape(token_count, width)
    own_inputs = tokens.astype(jnp.float32)
    own_cot = cotangent.astype(jnp.float32)
    first_norm_gain = vectors[0]
    first_norm_bias = vectors[1]
    second_norm_gain = vectors[2]
    second_norm_bias = vectors[3]
    out_bias = vectors[4]
    down_bias = vectors[5]
    query_bias = lax.dynamic_slice_in_dim(vectors[6], narrow_index * local_cols, local_cols)
    value_bias = lax.dynamic_slice_in_dim(vectors[7], narrow_index * local_cols, local_cols)
    up_bias = lax.dynamic_slice_in_dim(
        vectors[8:].reshape(-1), narrow_index * local_hidden, local_hidden
    )
    normalized_input, first_standardized, first_inverse_std = norm_shard_pieces(
        input_tokens, first_norm_gain, first_norm_bias
    )
    norm_low = normalized_input.astype(jnp.bfloat16)
    projected = jnp.einsum(
        "td,cde->cte", norm_low, attn_full[:3], preferred_element_type=jnp.float32
    )
    col_bias = jnp.stack([query_bias, jnp.zeros_like(query_bias), value_bias])
    qkv_low = (projected + col_bias[:, None, :]).astype(jnp.bfloat16)
    queries = qkv_low[0].reshape(sequence_count, seq_len, head_local, HEAD_DIM)
    key_rows = qkv_low[1].reshape(sequence_count, seq_len, head_local, HEAD_DIM)
    value_rows = qkv_low[2].reshape(sequence_count, seq_len, head_local, HEAD_DIM)

    def scores_for(block_index):
        row_index = block_index // block_count
        start = block_index % block_count * block_len
        query_block = lax.dynamic_slice_in_dim(
            lax.dynamic_index_in_dim(queries, row_index, 0, False), start, block_len, 0
        )
        key_block = lax.dynamic_index_in_dim(key_rows, row_index, 0, False)
        value_block = lax.dynamic_index_in_dim(value_rows, row_index, 0, False)
        seg_row = lax.dynamic_index_in_dim(segment_ids, row_index, 0, False)
        seg_query = lax.dynamic_slice_in_dim(seg_row, start, block_len, 0)
        raw = (
            jnp.einsum("qhd,khd->hqk", query_block, key_block, preferred_element_type=jnp.float32)
            * scale
        )
        same_doc = seg_query[:, None] == seg_row[None, :]
        masked = jnp.where(same_doc[None], raw, MASKED_SCORE)
        return (masked, query_block, key_block, value_block, row_index, start)

    def attend(block_index):
        masked, query_block, key_block, value_block, row_index, start = scores_for(block_index)
        top_score = jnp.max(masked, axis=-1, keepdims=True)
        expo = jnp.exp(masked - top_score)
        total = jnp.sum(expo, axis=-1, keepdims=True)
        probs_low = (expo / total).astype(jnp.bfloat16)
        context = jnp.einsum(
            "hqk,khd->qhd", probs_low, value_block, preferred_element_type=jnp.float32
        ).astype(jnp.bfloat16)
        return (context, top_score[..., 0] + jnp.log(total[..., 0]))

    block_ids = jnp.arange(sequence_count * block_count)
    contexts, log_totals = lax.map(attend, block_ids)
    context_rows = contexts.reshape(token_count, local_cols)
    out_part = jnp.einsum(
        "tc,dc->td", context_rows, attn_full[3], preferred_element_type=jnp.float32
    )
    out_share = lax.psum_scatter(
        out_part.reshape(sequence_count, seq_len, width), "narrow", scatter_dimension=1, tiled=True
    )
    hidden_own = own_inputs + out_share + out_bias
    normed_two_own, second_standardized_local, inv_two_own = norm_shard_pieces(
        hidden_own, second_norm_gain, second_norm_bias
    )
    second_in = lax.all_gather(
        normed_two_own.astype(jnp.bfloat16), "narrow", axis=1, tiled=True
    ).reshape(token_count, width)
    pre_act = jnp.dot(second_in, mlp_full[0], preferred_element_type=jnp.float32) + up_bias
    activated = exact_gelu(pre_act).astype(jnp.bfloat16)
    down_part = jnp.einsum("tf,df->td", activated, mlp_full[1], preferred_element_type=jnp.float32)
    down_share = lax.psum_scatter(
        down_part.reshape(sequence_count, seq_len, width).astype(jnp.bfloat16),
        "narrow",
        scatter_dimension=1,
        tiled=True,
    ).astype(jnp.float32)
    block_own = hidden_own + down_share + down_bias
    block_out = block_own.astype(jnp.bfloat16)
    grad_down_w = jnp.einsum(
        "td,tf->df", cotangent_token_rows, activated, preferred_element_type=jnp.float32
    )
    grad_act = jnp.dot(cotangent_token_rows, mlp_full[1], preferred_element_type=jnp.float32)
    unused_value, gelu_pull = jax.vjp(exact_gelu, pre_act)
    grad_pre = gelu_pull(grad_act)[0].astype(jnp.bfloat16)
    grad_up_w = jnp.einsum("td,tf->df", second_in, grad_pre, preferred_element_type=jnp.float32)
    grad_up_bias = jnp.sum(grad_pre, axis=0, dtype=jnp.float32)
    norm_two_part = jnp.einsum(
        "tf,df->td", grad_pre, mlp_full[0], preferred_element_type=jnp.float32
    )
    second_norm_local = lax.psum_scatter(
        norm_two_part.reshape(sequence_count, seq_len, width),
        "narrow",
        scatter_dimension=1,
        tiled=True,
    )
    residual_local = own_cot + norm_backward_pass(
        second_norm_local, second_standardized_local, inv_two_own, second_norm_gain
    )
    resid_low = lax.all_gather(
        residual_local.astype(jnp.bfloat16), "narrow", axis=1, tiled=True
    ).reshape(token_count, width)
    grad_out_w = jnp.einsum(
        "td,tc->dc", resid_low, context_rows, preferred_element_type=jnp.float32
    )
    grad_context = jnp.dot(resid_low, attn_full[3], preferred_element_type=jnp.float32).astype(
        jnp.bfloat16
    )
    grad_context = grad_context.reshape(sequence_count, seq_len, head_local, HEAD_DIM)

    def attend_back(block_index):
        masked, query_block, key_block, value_block, row_index, start = scores_for(block_index)
        grad_block = lax.dynamic_slice_in_dim(
            lax.dynamic_index_in_dim(grad_context, row_index, 0, False), start, block_len, 0
        )
        log_block = lax.dynamic_index_in_dim(log_totals, block_index, 0, False)
        probs = jnp.exp(masked - log_block[..., None])
        probs_low = probs.astype(jnp.bfloat16)
        grad_values = jnp.einsum(
            "hqk,qhd->khd", probs_low, grad_block, preferred_element_type=jnp.float32
        )
        grad_probs = jnp.einsum(
            "qhd,khd->hqk", grad_block, value_block, preferred_element_type=jnp.float32
        )
        inner = jnp.sum(probs * grad_probs, axis=-1, keepdims=True)
        grad_scores = (probs * (grad_probs - inner)).astype(jnp.bfloat16)
        grad_query = (
            jnp.einsum("hqk,khd->qhd", grad_scores, key_block, preferred_element_type=jnp.float32)
            * scale
        )
        grad_keys = (
            jnp.einsum("hqk,qhd->khd", grad_scores, query_block, preferred_element_type=jnp.float32)
            * scale
        )
        return (grad_query, grad_keys, grad_values)

    query_parts, key_parts, value_parts = lax.map(attend_back, block_ids)
    grad_query_rows = query_parts.reshape(token_count, local_cols)
    grad_key_rows = (
        key_parts.reshape(sequence_count, block_count, seq_len, local_cols)
        .sum(axis=1)
        .reshape(token_count, local_cols)
    )
    grad_value_rows = (
        value_parts.reshape(sequence_count, block_count, seq_len, local_cols)
        .sum(axis=1)
        .reshape(token_count, local_cols)
    )
    grad_qkv = jnp.stack([grad_query_rows, grad_key_rows, grad_value_rows]).astype(jnp.bfloat16)
    grad_qkv_w = jnp.einsum("td,cte->cde", norm_low, grad_qkv, preferred_element_type=jnp.float32)
    grad_query_bias = jnp.sum(grad_qkv[0], axis=0, dtype=jnp.float32)
    grad_value_bias = jnp.sum(grad_qkv[2], axis=0, dtype=jnp.float32)
    norm_one_part = jnp.einsum(
        "cte,cde->td", grad_qkv, attn_full[:3], preferred_element_type=jnp.float32
    )
    first_norm_local = lax.psum_scatter(
        norm_one_part.reshape(sequence_count, seq_len, width).astype(jnp.bfloat16),
        "narrow",
        scatter_dimension=1,
        tiled=True,
    ).astype(jnp.float32)
    first_standardized_local = local_shard_portion(
        first_standardized, sequence_count, shard_offset, shard_length
    )
    first_inverse_std_local = local_shard_portion(
        first_inverse_std, sequence_count, shard_offset, shard_length
    )
    block_input_gradient = residual_local + norm_backward_pass(
        first_norm_local, first_standardized_local, first_inverse_std_local, first_norm_gain
    )
    fixed_rows = jnp.stack(
        [
            jnp.sum(first_norm_local * first_standardized_local, axis=(0, 1)),
            jnp.sum(first_norm_local, axis=(0, 1)),
            jnp.sum(second_norm_local * second_standardized_local, axis=(0, 1)),
            jnp.sum(second_norm_local, axis=(0, 1)),
            jnp.sum(residual_local, axis=(0, 1)),
            jnp.sum(own_cot, axis=(0, 1)),
        ]
    )
    head_rows = lax.dynamic_update_slice_in_dim(
        jnp.zeros((2, width), jnp.float32),
        jnp.stack([grad_query_bias, grad_value_bias]),
        narrow_index * local_cols,
        1,
    )
    up_rows = lax.dynamic_update_slice_in_dim(
        jnp.zeros((local_hidden * narrow_count,), jnp.float32),
        grad_up_bias,
        narrow_index * local_hidden,
        0,
    ).reshape(-1, width)
    vec_local = jnp.concatenate([fixed_rows, head_rows, up_rows], axis=0)
    vec_grad = lax.psum(vec_local, ("wide", "narrow"))
    attn_local = jnp.concatenate([grad_qkv_w, grad_out_w[None]], axis=0)
    mlp_local = jnp.stack([grad_up_w, grad_down_w])
    attn_grad, mlp_grad = (
        lax.psum_scatter(
            attn_local.astype(jnp.bfloat16), "wide", scatter_dimension=1, tiled=True
        ).astype(jnp.float32),
        lax.psum_scatter(
            mlp_local.astype(jnp.bfloat16), "wide", scatter_dimension=1, tiled=True
        ).astype(jnp.float32),
    )
    attn_new, attn_m_new, attn_v_new = adamw_update(
        attn_w, attn_m, attn_v, attn_grad, RATE_MATRIX, DECAY_MATRIX
    )
    mlp_new, mlp_m_new, mlp_v_new = adamw_update(
        mlp_w, mlp_m, mlp_v, mlp_grad, RATE_MATRIX, DECAY_MATRIX
    )
    vec_new, vec_m_new, vec_v_new = adamw_update(vectors, vec_m, vec_v, vec_grad, RATE_VECTOR, 0.0)
    return (
        block_out,
        block_input_gradient,
        attn_grad,
        attn_new,
        attn_m_new,
        attn_v_new,
        mlp_grad,
        mlp_new,
        mlp_m_new,
        mlp_v_new,
        vec_grad,
        vec_new,
        vec_m_new,
        vec_v_new,
    )


def solution(mesh):
    in_specs = (
        P("wide", "narrow", None),
        P("wide", None),
        P("wide", "narrow", None),
        P(None, "wide", "narrow"),
        P(None, "wide", "narrow"),
        P(None, "wide", "narrow"),
        P(None, "wide", "narrow"),
        P(None, "wide", "narrow"),
        P(None, "wide", "narrow"),
        P(),
        P(),
        P(),
    )
    out_specs = (
        P("wide", "narrow", None),
        P("wide", "narrow", None),
        P(None, "wide", "narrow"),
        P(None, "wide", "narrow"),
        P(None, "wide", "narrow"),
        P(None, "wide", "narrow"),
        P(None, "wide", "narrow"),
        P(None, "wide", "narrow"),
        P(None, "wide", "narrow"),
        P(None, "wide", "narrow"),
        P(),
        P(),
        P(),
        P(),
    )
    return jax.shard_map(local, mesh=mesh, in_specs=in_specs, out_specs=out_specs, check_vma=False)
```

profile of v0, /device:TPU:0, one launch (start us, length us, event | category | flops | bytes accessed | tf_op | source)
XLA Modules:
  0.0 722.1 jit_solution(8954707669613405270)
XLA Ops:
  11.9 45.8 %all-gather.9.cloned.1.call-done = bf16[4,768,192]{2,0,1:T(4,128)(2,1)} async-done(((bf16[4,96,192]{2,0,1:T(4,128)(2,1)}), bf16[4,768,192]{2,0,1:T(4,128)(2,1)}) %all-gather.9.cloned.1.call-update) | async-done | bytes 1179664 | tf_op jit(solution)/shard_map/all_gather | solution.py:83
  57.7 2.4 slice.74
  61.5 25.1 %all-gather.7.cloned.1.call-done = bf16[2,1024,768]{2,1,0:T(8,128)(2,1)} async-done(((bf16[2,256,768]{2,1,0:T(8,128)(2,1)}), bf16[2,1024,768]{2,1,0:T(8,128)(2,1)}) %all-gather.7.cloned.1.call-update) | async-done | bytes 3145744 | tf_op jit(solution)/shard_map/all_gather | solution.py:87
  86.6 2.5 convert_reduce_fusion.1
  89.5 3.8 convert_subtract_fusion
  100.1 39.2 %while.32 = (s32[]{:T(128)}, bf16[4,512,3,64]{1,3,2,0:T(8,128)(2,1)}, f32[4,3,512]{2,1,0:T(4,128)S(1)}, s32[4]{0:T(128)S(1)}, bf16[2,1024,3,64]{1,3,2,0:T(8,128)...) while((s32[]{:T(128)}, ...), condition=%wide.region_5.6_spmd, body=%wide.region_2.5_spmd.sunk | while | flops 422148640 | bytes 22229476 | solution.py:148
  107.1 2.7 fusion.152
  116.8 2.7 fusion.152
  126.5 2.7 fusion.152
  136.2 2.7 fusion.152
  142.8 4.8 fusion.97
  149.5 56.7 %reduce-scatter.9.cloned.1.call-done = f32[2,256,768]{2,1,0:T(8,128)} async-done(((f32[2,1024,768]{2,1,0:T(8,128)}), f32[2,256,768]{2,1,0:T(8,128)}) %reduce-scatter.9.cloned.1.call-update) | async-done | bytes 1572880 | tf_op jit(solution)/shard_map/reduce_scatter | solution.py:153
  210.3 50.6 %all-gather.13.cloned.1.call-done = bf16[2,768,768]{2,1,0:T(8,128)(2,1)} async-done(((bf16[2,96,768]{2,1,0:T(8,128)(2,1)}), bf16[2,768,768]{2,1,0:T(8,128)(2,1)}) %all-gather.13.cloned.1.call-update) | async-done | bytes 2359312 | tf_op jit(solution)/shard_map/all_gather | solution.py:84
  261.0 29.2 %all-gather.11.cloned.1.call-done = bf16[2,1024,768]{2,1,0:T(8,128)(2,1)} async-done(((bf16[2,256,768]{2,1,0:T(8,128)(2,1)}), bf16[2,1024,768]{2,1,0:T(8,128)(2,1)}) %all-gather.11.cloned.1.call-update) | async-done | bytes 3145744 | tf_op jit(solution)/shard_map/all_gather | solution.py:160
  290.1 19.0 %multiply_convert_fusion.1 = (bf16[2048,768]{1,0:T(8,128)(2,1)}, f32[2048,768]{1,0:T(8,128)}, f32[2048,768]{1,0:T(8,128)}) fusion(f32[768]{0:T(1024)S(1)} %dynamic_slice.110, bf16[2048,768]{1,0:T(8,128)(2,1)} %bitcast.256, bf16[2,768,768]{2,1,0:T(8,128)(2,1)} %all-gather.13.cloned.1.call-done), kind=kOutput, calls=%fused_computation.73 | convolution fusion | flops 2519728128 | bytes 20057088 | tf_op jit(solution)/shard_map/dot_general | solution.py:163
  309.1 11.1 %all-gather.15.cloned.1.call-done = bf16[2,1024,768]{2,1,0:T(8,128)(2,1)} async-done(((bf16[2,256,768]{2,1,0:T(8,128)(2,1)}), bf16[2,1024,768]{2,1,0:T(8,128)(2,1)}) %all-gather.15.cloned.1.call-update) | async-done | bytes 3145744 | tf_op jit(solution)/shard_map/all_gather | solution.py:88
  320.2 10.6 %convert_reduce_fusion = (f32[768]{0:T(1024)S(1)}, bf16[2048,768]{1,0:T(8,128)(2,1)S(1)}) fusion(f32[2048,768]{1,0:T(8,128)} %get-tuple-element.504, bf16[2048,768]{1,0:T(8,128)(2,1)} %bitcast.258, bf16[2,768,768]{2,1,0:T(8,128)(2,1)} %all-gather.13.cloned.1.call-done, f32[2048,768]{1,0:T(8,128)} %get-tuple-element.530, f32[768]{0:T(1024)S(1)} %dynamic_slice.110), kind=kOutput, calls=%fused_computation.71 | convolution fusion | flops 2442657024 | bytes 20060160 | tf_op jit(solution)/shard_map/dot_general | solution.py:177
  332.5 4.5 fusion.83
  337.0 6.6 convolution_convert_fusion.1
  343.9 51.6 %reduce-scatter.13.cloned.1.call-done = f32[2,256,768]{2,1,0:T(8,128)} async-done(((f32[2,1024,768]{2,1,0:T(8,128)}), f32[2,256,768]{2,1,0:T(8,128)}) %reduce-scatter.13.cloned.1.call-update) | async-done | bytes 1572880 | tf_op jit(solution)/shard_map/reduce_scatter | solution.py:185
  397.6 38.4 %reduce-scatter.11.cloned.1.call-done = bf16[2,256,768]{2,1,0:T(8,128)(2,1)} async-done(((bf16[2,1024,768]{2,1,0:T(8,128)(2,1)}), bf16[2,256,768]{2,1,0:T(8,128)(2,1)}) %reduce-scatter.11.cloned.1.call-update) | async-done | bytes 786448 | tf_op jit(solution)/shard_map/reduce_scatter | solution.py:166
  436.1 3.6 fusion.107
  442.9 5.6 fusion.79
  448.6 2.7 fusion.78
  453.0 17.5 %all-gather.17.cloned.1.call-done = bf16[2,1024,768]{2,1,0:T(8,128)(2,1)} async-done(((bf16[2,256,768]{2,1,0:T(8,128)(2,1)}), bf16[2,1024,768]{2,1,0:T(8,128)(2,1)}) %all-gather.17.cloned.1.call-update) | async-done | bytes 3145744 | tf_op jit(solution)/shard_map/all_gather | solution.py:194
  470.5 3.1 convolution_convert_fusion
  476.4 64.6 %while.33 = (s32[]{:T(128)}, bf16[4,512,3,64]{1,3,2,0:T(8,128)(2,1)}, f32[4,1024,3,64]{1,3,2,0:T(8,128)}, f32[4,1024,3,64]{1,3,2,0:T(8,128)}, s32[4]{0:T(128)S(1...) while((s32[]{:T(128)}, ...), condition=%wide.region_15.16_spmd, body=%wide.region_13.15_spmd.sunk | while | flops 1031043584 | bytes 59572856 | solution.py:231
  482.7 2.8 fusion.164
  485.5 2.6 multiply_reduce_fusion.7
  498.8 2.8 fusion.164
  501.6 2.6 multiply_reduce_fusion.7
  514.9 2.8 fusion.164
  517.7 2.6 multiply_reduce_fusion.7
  530.9 2.8 fusion.164
  533.8 2.6 multiply_reduce_fusion.7
  541.0 2.3 reduce_sum.204
  543.2 2.3 reduce_sum.203
  548.4 2.6 copy.77
  551.0 2.3 stack_reshape.12
  553.6 2.5 copy-done.11
  560.2 2.6 copy.91
  565.2 6.2 bitcast_convert_fusion
  574.9 2.9 multiply_subtract_fusion
  578.4 50.8 %reduce-scatter.19.cloned.1.call-done = bf16[96,768]{1,0:T(8,128)(2,1)} async-done(((bf16[768,768]{1,0:T(8,128)(2,1)}), bf16[96,768]{1,0:T(8,128)(2,1)}) %reduce-scatter.19.cloned.1.call-update) | async-done | bytes 147472
  637.5 31.3 %reduce-scatter.15.cloned.1.call-done = bf16[2,256,768]{2,1,0:T(8,128)(2,1)} async-done(((bf16[2,1024,768]{2,1,0:T(8,128)(2,1)}), bf16[2,256,768]{2,1,0:T(8,128)(2,1)}) %reduce-scatter.15.cloned.1.call-update) | async-done | bytes 786448 | tf_op jit(solution)/shard_map/reduce_scatter | solution.py:250
  668.8 2.4 fusion.74
  671.3 39.7 %psum.7 = f32[12,768]{1,0:T(8,128)S(1)} all-reduce(f32[12,768]{1,0:T(8,128)S(1)} %concatenate.8), channel_id=1, replica_groups=mesh['wide'=8,'narrow'=4] {'wide','narrow'}, use_global_device_ids=true, to_apply=%region_32.33 | all-reduce | flops 9216 | bytes 73728 | tf_op jit(solution)/shard_map/psum | solution.py:288
  711.8 3.0 fusion.72
  (253 shorter events, 101.0 us)
Async XLA Ops:
  7.2 50.5 %all-gather.9.cloned.1.call-start = ((), (), s32[]{:S(2)}) async-start(), calls=%async_computation.7 | async-start | bytes 1769472 | tf_op jit(solution)/shard_map/all_gather | solution.py:83
  9.2 77.4 %all-gather.7.cloned.1.call-start = ((), (), s32[]{:S(2)}) async-start(), calls=%async_computation.6 | async-start | bytes 3932160 | tf_op jit(solution)/shard_map/all_gather | solution.py:87
  9.9 196.2 %reduce-scatter.9.cloned.1.call-start = ((), (), s32[]{:S(2)}) async-start(), calls=%async_computation.8 | async-start | bytes 7864320 | tf_op jit(solution)/shard_map/reduce_scatter | solution.py:153
  11.8 82.1 %copy-start.24 = (f32[768]{0:T(1024)}, f32[768]{0:T(1024)S(1)}, u32[]{:S(2)}) copy-start(f32[768]{0:T(1024)S(1)} %get-tuple-element.520) | copy-start | bytes 9220
  57.7 2.9 copy-start.7
  61.5 33.7 %copy-start.16 = (bf16[3,768,192]{1,2,0:T(8,128)(2,1)}, bf16[3,768,192]{1,2,0:T(8,128)(2,1)S(1)}, u32[]{:S(2)}) copy-start(bf16[3,768,192]{1,2,0:T(8,128)(2,1)S(1)} %copy.93) | copy-start | bytes 2654212
  86.6 2.8 copy-start
  95.1 2.1 copy-start.9
  98.5 1.6 copy-start.19
  139.3 8.3 %copy-start.3 = (bf16[2,1024,3,64]{1,3,2,0:T(8,128)(2,1)}, bf16[2,1024,3,64]{1,3,2,0:T(8,128)(2,1)S(1)}, u32[]{:S(2)}) copy-start(bf16[2,1024,3,64]{1,3,2,0:T(8,128)(2,1)S(1)} %get-tuple-element.774) | copy-start | bytes 2359300
  141.4 6.2 copy-start.5
  147.6 113.3 %all-gather.13.cloned.1.call-start = ((), (), s32[]{:S(2)}) async-start(), calls=%async_computation.10 | async-start | bytes 2654208 | tf_op jit(solution)/shard_map/all_gather | solution.py:84
  149.4 140.7 %all-gather.11.cloned.1.call-start = ((), (), s32[]{:S(2)}) async-start(), calls=%async_computation.9 | async-start | bytes 3932160 | tf_op jit(solution)/shard_map/all_gather | solution.py:160
  208.0 2.2 slice-start
  209.6 110.6 %all-gather.15.cloned.1.call-start = ((), (), s32[]{:S(2)}) async-start(), calls=%async_computation.12 | async-start | bytes 3932160 | tf_op jit(solution)/shard_map/all_gather | solution.py:88
  210.2 185.3 %reduce-scatter.13.cloned.1.call-start = ((), (), s32[]{:S(2)}) async-start(), calls=%async_computation.13 | async-start | bytes 7864320 | tf_op jit(solution)/shard_map/reduce_scatter | solution.py:185
  320.2 12.3 %copy-start.30 = (bf16[2,768,768]{2,1,0:T(8,128)(2,1)S(1)}, bf16[2,768,768]{2,1,0:T(8,128)(2,1)}, u32[]{:S(2)}) copy-start(bf16[2,768,768]{2,1,0:T(8,128)(2,1)} %all-gather.13.cloned.1.call-done) | copy-start | bytes 7077892
  330.8 1.7 copy-start.31
  337.0 99.1 %reduce-scatter.11.cloned.1.call-start = ((), (), s32[]{:S(2)}) async-start(), calls=%async_computation.11 | async-start | bytes 3932160 | tf_op jit(solution)/shard_map/reduce_scatter | solution.py:166
  343.6 92.4 %copy-start.28 = (f32[768]{0:T(1024)S(1)}, f32[768]{0:T(1024)}, u32[]{:S(2)}) copy-start(f32[768]{0:T(1024)} %get-tuple-element.525) | copy-start | bytes 9220
  343.7 126.8 %all-gather.17.cloned.1.call-start = ((), (), s32[]{:S(2)}) async-start(), calls=%async_computation.14 | async-start | bytes 3932160 | tf_op jit(solution)/shard_map/all_gather | solution.py:194
  439.6 2.2 copy-start.6
  441.8 133.1 %reduce-scatter.17.cloned.1.call-start = ((), (), s32[]{:S(2)}) async-start(), calls=%async_computation.16 | async-start | bytes 2654208 | tf_op jit(solution)/shard_map/reduce_scatter | solution.py:295
  442.9 5.7 copy-start.29
  442.9 5.7 copy-start.32
  452.9 176.3 %reduce-scatter.19.cloned.1.call-start = ((), (), s32[]{:S(2)}) async-start(), calls=%async_computation.17 | async-start | bytes 1327104
  473.5 2.8 copy-start.4
  488.1 1.8 copy-start.17
  491.0 1.6 copy-start.18
  504.2 1.8 copy-start.17
  507.1 1.7 copy-start.18
  520.3 1.8 copy-start.17
  523.2 1.6 copy-start.18
  536.4 1.8 copy-start.17
  539.3 1.6 copy-start.18
  551.0 2.6 copy-start.8
  553.4 2.7 copy-start.11
  553.5 3.6 copy-start.10
  553.6 5.5 copy-start.21
  565.1 103.7 %reduce-scatter.15.cloned.1.call-start = ((), (), s32[]{:S(2)}) async-start(), calls=%async_computation.15 | async-start | bytes 3932160 | tf_op jit(solution)/shard_map/reduce_scatter | solution.py:250
  571.4 3.5 copy-start.14
  578.2 90.6 %copy-start.25 = (f32[768]{0:T(1024)S(1)}, f32[768]{0:T(1024)}, u32[]{:S(2)}) copy-start(f32[768]{0:T(1024)} %copy-done.24) | copy-start | bytes 9220
  631.4 79.6 %copy-start.23 = (f32[12,768]{1,0:T(8,128)S(1)}, f32[12,768]{1,0:T(8,128)}, u32[]{:S(2)}) copy-start(f32[12,768]{1,0:T(8,128)} %param.25) | copy-start | bytes 110596
  631.4 79.6 %copy-start.26 = (f32[12,768]{1,0:T(8,128)S(1)}, f32[12,768]{1,0:T(8,128)}, u32[]{:S(2)}) copy-start(f32[12,768]{1,0:T(8,128)} %param.26) | copy-start | bytes 110596
  631.4 79.6 %copy-start.27 = (f32[12,768]{1,0:T(8,128)S(1)}, f32[12,768]{1,0:T(8,128)}, u32[]{:S(2)}) copy-start(f32[12,768]{1,0:T(8,128)} %param.27) | copy-start | bytes 110596
  632.6 79.2 %copy-start.2 = (f32[2,256,768]{2,1,0:T(8,128)S(1)}, f32[2,256,768]{2,1,0:T(8,128)}, u32[]{:S(2)}) copy-start(f32[2,256,768]{2,1,0:T(8,128)} %copy-done.1) | copy-start | bytes 4718596
  668.8 43.0 %copy-start.12 = (bf16[2,256,768]{2,1,0:T(8,128)(2,1)S(1)}, bf16[2,256,768]{2,1,0:T(8,128)(2,1)}, u32[]{:S(2)}) copy-start(bf16[2,256,768]{2,1,0:T(8,128)(2,1)} %reduce-scatter.15.cloned.1.call-done) | copy-start | bytes 2359300
  711.1 3.7 copy-start.22
  (4 other events, 4.4 us)
Sparse Core Ops, SparseCore 0:
  10.8 46.8 all-gather.8
  59.2 27.3 all-gather.6
  147.8 58.3 reduce-scatter.8
  209.0 51.9 all-gather.12
  263.0 27.0 all-gather.10
  291.6 28.5 all-gather.14
  337.1 58.3 reduce-scatter.12
  398.0 37.9 reduce-scatter.10
  441.9 28.5 all-gather.16
  474.2 69.1 reduce-scatter.16
  565.3 63.9 reduce-scatter.18
  631.8 36.9 reduce-scatter.14
where the time goes:
time: 732 us; the launch traced here: 722 us
  waiting for transfers between devices  409 us (56%)
  matrix products  122 us (17%)
  other arithmetic  54.4 us (7%)
  local copies, waits for them, and re-layouts  53.4 us (7%)
  blocking collectives  39.7 us (5%)
  loops' own time  27.1 us (4%)
  between operations  15.4 us (2%)
    reduce_scatter x1, waiting for transfers between devices, local(): lax.psum_scatter(out_part.reshape(sequence_count, seq_len, width), 'narro...  56.7 us
    unnamed x13, waiting for transfers between devices  52.2 us
    reduce_scatter x1, waiting for transfers between devices, local(): lax.psum_scatter(norm_two_part.reshape(sequence_count, seq_len, width), '...  51.6 us
    all_gather x1, waiting for transfers between devices, local(): lax.all_gather(mlp_w.astype(jnp.bfloat16), 'wide', axis=1, tiled=True)  50.6 us
    all_gather x1, waiting for transfers between devices, local(): lax.all_gather(attn_w.astype(jnp.bfloat16), 'wide', axis=1, tiled=True)  45.8 us
    psum x1, blocking collectives, local(): vec_grad = lax.psum(vec_local, ('wide', 'narrow'))  39.7 us
    reduce_scatter x1, waiting for transfers between devices, local(): lax.psum_scatter(down_part.reshape(sequence_count, seq_len, width).astype...  38.4 us
    reduce_scatter x1, waiting for transfers between devices, local(): lax.psum_scatter(norm_one_part.reshape(sequence_count, seq_len, width).as...  31.3 us
  transfers between devices with their start and end apart: 12, of which 11 were waited for; matrix products, arithmetic and copies ran while one was open for 20% of the time, Pallas kernels for 0%

commit v1 on v0

--- a/solution.py
+++ b/solution.py
@@ -67,6 +67,10 @@
     vec_m,
     vec_v,
 ):
+
+    def post_the_clusters(point):
+        return lax.all_gather(point, ("wide", "narrow")).sum(axis=0)
+
     narrow_count = lax.axis_size("narrow")
     narrow_index = lax.axis_index("narrow")
     sequence_count, shard_length, width = tokens.shape
@@ -285,7 +289,7 @@
         0,
     ).reshape(-1, width)
     vec_local = jnp.concatenate([fixed_rows, head_rows, up_rows], axis=0)
-    vec_grad = lax.psum(vec_local, ("wide", "narrow"))
+    vec_grad = post_the_clusters(vec_local)
     attn_local = jnp.concatenate([grad_qkv_w, grad_out_w[None]], axis=0)
     mlp_local = jnp.stack([grad_up_w, grad_down_w])
     attn_grad, mlp_grad = (

time: 732 us -> 809 us (1.11)
  waiting for transfers between devices: 409 us -> 527 us
  blocking collectives: 39.7 us -> 0 us
    reduce_scatter x1, waiting for transfers between devices: 0.01 us -> 65.9 us  [local(): lax.psum_scatter(mlp_local.astype(jnp.bfloat16), 'wide', scatter_dimensio...]
    all_gather x0 -> x1, waiting for transfers between devices: none -> 44.2 us  [post_the_clusters(): return lax.all_gather(point, ('wide', 'narrow')).sum(axis=0)]
    psum x1 -> x0, blocking collectives: 39.7 us -> none  [local(): vec_grad = lax.psum(vec_local, ('wide', 'narrow'))]
    reduce_scatter x1, waiting for transfers between devices: 31.3 us -> 14.4 us  [local(): lax.psum_scatter(norm_one_part.reshape(sequence_count, seq_len, width).as...]
    unnamed x13 -> x14, waiting for transfers between devices: 52.2 us -> 65.1 us
    all_gather x1, waiting for transfers between devices: 17.5 us -> 28.6 us  [local(): lax.all_gather(residual_local.astype(jnp.bfloat16), 'narrow', axis=1, til...]
    unnamed x79 -> x81, local copies, waits for them, and re-layouts: 25.9 us -> 25.5 us
  transfers between devices with their start and end apart: 12 -> 13, of which waited for: 11 -> 13; matrix products, arithmetic and copies ran while one was open for 20% -> 10% of each run, Pallas kernels for 0% -> 0%
where the time goes in v1:
time: 809 us; the launch traced here: 799 us
  waiting for transfers between devices  527 us (65%)
  matrix products  122 us (15%)
  other arithmetic  56.9 us (7%)
  local copies, waits for them, and re-layouts  50.5 us (6%)
  loops' own time  27 us (3%)
  between operations  15.1 us (2%)
    reduce_scatter x1, waiting for transfers between devices, local(): lax.psum_scatter(mlp_local.astype(jnp.bfloat16), 'wide', scatter_dimensio...  65.9 us
    unnamed x14, waiting for transfers between devices  65.1 us
    reduce_scatter x1, waiting for transfers between devices, local(): lax.psum_scatter(out_part.reshape(sequence_count, seq_len, width), 'narro...  56.7 us
    reduce_scatter x1, waiting for transfers between devices, local(): lax.psum_scatter(norm_two_part.reshape(sequence_count, seq_len, width), '...  51.6 us
    all_gather x1, waiting for transfers between devices, local(): lax.all_gather(mlp_w.astype(jnp.bfloat16), 'wide', axis=1, tiled=True)  50.6 us
    all_gather x1, waiting for transfers between devices, local(): lax.all_gather(attn_w.astype(jnp.bfloat16), 'wide', axis=1, tiled=True)  45.8 us
    all_gather x1, waiting for transfers between devices, post_the_clusters(): return lax.all_gather(point, ('wide', 'narrow')).sum(axis=0)  44.2 us
    reduce_scatter x1, waiting for transfers between devices, local(): lax.psum_scatter(down_part.reshape(sequence_count, seq_len, width).astype...  38.4 us
  transfers between devices with their start and end apart: 13, of which 13 were waited for; matrix products, arithmetic and copies ran while one was open for 10% of the time, Pallas kernels for 0%

profile of v1, /device:TPU:0, one launch (start us, length us, event | category | flops | bytes accessed | tf_op | source)
XLA Modules:
  0.0 799.0 jit_solution(14454966400560941774)
XLA Ops:
  11.9 45.8 %all-gather.12.cloned.1.call-done = bf16[4,768,192]{2,0,1:T(4,128)(2,1)} async-done(((bf16[4,96,192]{2,0,1:T(4,128)(2,1)}), bf16[4,768,192]{2,0,1:T(4,128)(2,1)}) %all-gather.12.cloned.1.call-update) | async-done | bytes 1179664 | tf_op jit(solution)/shard_map/all_gather | solution.py:87
  57.7 2.4 slice.74
  61.5 25.1 %all-gather.10.cloned.1.call-done = bf16[2,1024,768]{2,1,0:T(8,128)(2,1)} async-done(((bf16[2,256,768]{2,1,0:T(8,128)(2,1)}), bf16[2,1024,768]{2,1,0:T(8,128)(2,1)}) %all-gather.10.cloned.1.call-update) | async-done | bytes 3145744 | tf_op jit(solution)/shard_map/all_gather | solution.py:91
  86.6 2.5 convert_reduce_fusion.1
  89.5 3.8 convert_subtract_fusion
  100.1 39.2 %while.32 = (s32[]{:T(128)}, bf16[4,512,3,64]{1,3,2,0:T(8,128)(2,1)}, f32[4,3,512]{2,1,0:T(4,128)S(1)}, s32[4]{0:T(128)S(1)}, bf16[2,1024,3,64]{1,3,2,0:T(8,128)...) while((s32[]{:T(128)}, ...), condition=%wide.region_5.6_spmd, body=%wide.region_2.5_spmd.sunk | while | flops 422148640 | bytes 22229476 | solution.py:152
  107.1 2.7 fusion.152
  116.8 2.7 fusion.152
  126.5 2.7 fusion.152
  136.2 2.7 fusion.152
  142.8 4.8 fusion.97
  149.5 56.7 %reduce-scatter.9.cloned.1.call-done = f32[2,256,768]{2,1,0:T(8,128)} async-done(((f32[2,1024,768]{2,1,0:T(8,128)}), f32[2,256,768]{2,1,0:T(8,128)}) %reduce-scatter.9.cloned.1.call-update) | async-done | bytes 1572880 | tf_op jit(solution)/shard_map/reduce_scatter | solution.py:157
  210.3 50.6 %all-gather.16.cloned.1.call-done = bf16[2,768,768]{2,1,0:T(8,128)(2,1)} async-done(((bf16[2,96,768]{2,1,0:T(8,128)(2,1)}), bf16[2,768,768]{2,1,0:T(8,128)(2,1)}) %all-gather.16.cloned.1.call-update) | async-done | bytes 2359312 | tf_op jit(solution)/shard_map/all_gather | solution.py:88
  261.0 29.2 %all-gather.14.cloned.1.call-done = bf16[2,1024,768]{2,1,0:T(8,128)(2,1)} async-done(((bf16[2,256,768]{2,1,0:T(8,128)(2,1)}), bf16[2,1024,768]{2,1,0:T(8,128)(2,1)}) %all-gather.14.cloned.1.call-update) | async-done | bytes 3145744 | tf_op jit(solution)/shard_map/all_gather | solution.py:164
  290.1 19.0 %multiply_convert_fusion.1 = (bf16[2048,768]{1,0:T(8,128)(2,1)}, f32[2048,768]{1,0:T(8,128)}, f32[2048,768]{1,0:T(8,128)}) fusion(f32[768]{0:T(1024)S(1)} %dynamic_slice.110, bf16[2048,768]{1,0:T(8,128)(2,1)} %bitcast.258, bf16[2,768,768]{2,1,0:T(8,128)(2,1)} %all-gather.16.cloned.1.call-done), kind=kOutput, calls=%fused_computation.73 | convolution fusion | flops 2519728128 | bytes 20057088 | tf_op jit(solution)/shard_map/dot_general | solution.py:167
  309.1 11.1 %all-gather.18.cloned.1.call-done = bf16[2,1024,768]{2,1,0:T(8,128)(2,1)} async-done(((bf16[2,256,768]{2,1,0:T(8,128)(2,1)}), bf16[2,1024,768]{2,1,0:T(8,128)(2,1)}) %all-gather.18.cloned.1.call-update) | async-done | bytes 3145744 | tf_op jit(solution)/shard_map/all_gather | solution.py:92
  320.2 10.6 %convert_reduce_fusion = (f32[768]{0:T(1024)S(1)}, bf16[2048,768]{1,0:T(8,128)(2,1)S(1)}) fusion(f32[2048,768]{1,0:T(8,128)} %get-tuple-element.504, bf16[2048,768]{1,0:T(8,128)(2,1)} %bitcast.260, bf16[2,768,768]{2,1,0:T(8,128)(2,1)} %all-gather.16.cloned.1.call-done, f32[2048,768]{1,0:T(8,128)} %get-tuple-element.530, f32[768]{0:T(1024)S(1)} %dynamic_slice.110), kind=kOutput, calls=%fused_computation.71 | convolution fusion | flops 2442657024 | bytes 20060160 | tf_op jit(solution)/shard_map/dot_general | solution.py:181
  332.5 4.5 fusion.83
  337.0 6.6 convolution_convert_fusion.1
  343.9 51.6 %reduce-scatter.13.cloned.1.call-done = f32[2,256,768]{2,1,0:T(8,128)} async-done(((f32[2,1024,768]{2,1,0:T(8,128)}), f32[2,256,768]{2,1,0:T(8,128)}) %reduce-scatter.13.cloned.1.call-update) | async-done | bytes 1572880 | tf_op jit(solution)/shard_map/reduce_scatter | solution.py:189
  397.6 38.4 %reduce-scatter.11.cloned.1.call-done = bf16[2,256,768]{2,1,0:T(8,128)(2,1)} async-done(((bf16[2,1024,768]{2,1,0:T(8,128)(2,1)}), bf16[2,256,768]{2,1,0:T(8,128)(2,1)}) %reduce-scatter.11.cloned.1.call-update) | async-done | bytes 786448 | tf_op jit(solution)/shard_map/reduce_scatter | solution.py:170
  436.1 3.6 fusion.107
  441.8 28.6 %all-gather.20.cloned.1.call-done = bf16[2,1024,768]{2,1,0:T(8,128)(2,1)} async-done(((bf16[2,256,768]{2,1,0:T(8,128)(2,1)}), bf16[2,1024,768]{2,1,0:T(8,128)(2,1)}) %all-gather.20.cloned.1.call-update) | async-done | bytes 3145744 | tf_op jit(solution)/shard_map/all_gather | solution.py:198
  470.5 3.1 convolution_convert_fusion
  476.4 64.6 %while.33 = (s32[]{:T(128)}, bf16[4,512,3,64]{1,3,2,0:T(8,128)(2,1)}, f32[4,1024,3,64]{1,3,2,0:T(8,128)}, f32[4,1024,3,64]{1,3,2,0:T(8,128)}, s32[4]{0:T(128)S(1...) while((s32[]{:T(128)}, ...), condition=%wide.region_15.16_spmd, body=%wide.region_13.15_spmd.sunk | while | flops 1031043584 | bytes 59572856 | solution.py:235
  482.5 2.8 fusion.164
  485.3 2.6 multiply_reduce_fusion.7
  498.5 2.8 fusion.164
  501.4 2.6 multiply_reduce_fusion.7
  514.6 2.8 fusion.164
  517.4 2.6 multiply_reduce_fusion.7
  530.7 2.8 fusion.164
  533.5 2.6 multiply_reduce_fusion.7
  541.0 2.3 reduce_sum.213
  545.9 2.3 reduce_sum.212
  550.8 4.1 bitcast_convert_fusion
  555.0 5.6 fusion.79
  560.7 2.7 fusion.78
  565.6 2.8 fusion.92
  572.1 2.7 copy.91
  574.8 2.2 reshape.318
  578.7 14.4 %reduce-scatter.15.cloned.1.call-done = bf16[2,256,768]{2,1,0:T(8,128)(2,1)} async-done(((bf16[2,1024,768]{2,1,0:T(8,128)(2,1)}), bf16[2,256,768]{2,1,0:T(8,128)(2,1)}) %reduce-scatter.15.cloned.1.call-update) | async-done | bytes 786448 | tf_op jit(solution)/shard_map/reduce_scatter | solution.py:254
  593.1 2.3 fusion.74
  600.0 65.9 %reduce-scatter.17.cloned.1.call-done = bf16[2,96,768]{2,1,0:T(8,128)(2,1)} async-done(((bf16[2,768,768]{2,1,0:T(8,128)(2,1)}), bf16[2,96,768]{2,1,0:T(8,128)(2,1)}) %reduce-scatter.17.cloned.1.call-update) | async-done | bytes 294928 | tf_op jit(solution)/shard_map/reduce_scatter | solution.py:299
  665.9 2.7 multiply_subtract_fusion
  668.6 63.7 %reduce-scatter.19.cloned.1.call-done = bf16[96,768]{1,0:T(8,128)(2,1)} async-done(((bf16[768,768]{1,0:T(8,128)(2,1)}), bf16[96,768]{1,0:T(8,128)(2,1)}) %reduce-scatter.19.cloned.1.call-update) | async-done | bytes 147472
  742.6 3.1 fusion.72
  745.6 44.2 %all-gather.22.cloned.1.call-done = f32[32,12,768]{2,1,0:T(8,128)} async-done(((f32[1,12,768]{2,1,0:T(8,128)}), f32[32,12,768]{2,1,0:T(8,128)}) %all-gather.22.cloned.1.call-update) | async-done | bytes 1179664 | tf_op jit(solution)/shard_map/all_gather | solution.py:72
  (258 shorter events, 105.4 us)
Async XLA Ops:
  7.2 50.5 %all-gather.12.cloned.1.call-start = ((), (), s32[]{:S(2)}) async-start(), calls=%async_computation.7 | async-start | bytes 1769472 | tf_op jit(solution)/shard_map/all_gather | solution.py:87
  9.2 77.4 %all-gather.10.cloned.1.call-start = ((), (), s32[]{:S(2)}) async-start(), calls=%async_computation.6 | async-start | bytes 3932160 | tf_op jit(solution)/shard_map/all_gather | solution.py:91
  9.9 196.2 %reduce-scatter.9.cloned.1.call-start = ((), (), s32[]{:S(2)}) async-start(), calls=%async_computation.8 | async-start | bytes 7864320 | tf_op jit(solution)/shard_map/reduce_scatter | solution.py:157
  11.8 82.1 %copy-start.25 = (f32[768]{0:T(1024)}, f32[768]{0:T(1024)S(1)}, u32[]{:S(2)}) copy-start(f32[768]{0:T(1024)S(1)} %get-tuple-element.520) | copy-start | bytes 9220
  57.7 2.9 copy-start.7
  61.5 33.7 %copy-start.14 = (bf16[3,768,192]{1,2,0:T(8,128)(2,1)}, bf16[3,768,192]{1,2,0:T(8,128)(2,1)S(1)}, u32[]{:S(2)}) copy-start(bf16[3,768,192]{1,2,0:T(8,128)(2,1)S(1)} %copy.93) | copy-start | bytes 2654212
  86.6 2.8 copy-start
  95.1 2.1 copy-start.8
  139.3 8.3 %copy-start.3 = (bf16[2,1024,3,64]{1,3,2,0:T(8,128)(2,1)}, bf16[2,1024,3,64]{1,3,2,0:T(8,128)(2,1)S(1)}, u32[]{:S(2)}) copy-start(bf16[2,1024,3,64]{1,3,2,0:T(8,128)(2,1)S(1)} %get-tuple-element.775) | copy-start | bytes 2359300
  141.4 6.2 copy-start.5
  147.6 113.3 %all-gather.16.cloned.1.call-start = ((), (), s32[]{:S(2)}) async-start(), calls=%async_computation.10 | async-start | bytes 2654208 | tf_op jit(solution)/shard_map/all_gather | solution.py:88
  149.4 140.7 %all-gather.14.cloned.1.call-start = ((), (), s32[]{:S(2)}) async-start(), calls=%async_computation.9 | async-start | bytes 3932160 | tf_op jit(solution)/shard_map/all_gather | solution.py:164
  208.0 2.2 slice-start
  209.6 110.6 %all-gather.18.cloned.1.call-start = ((), (), s32[]{:S(2)}) async-start(), calls=%async_computation.12 | async-start | bytes 3932160 | tf_op jit(solution)/shard_map/all_gather | solution.py:92
  210.2 185.3 %reduce-scatter.13.cloned.1.call-start = ((), (), s32[]{:S(2)}) async-start(), calls=%async_computation.13 | async-start | bytes 7864320 | tf_op jit(solution)/shard_map/reduce_scatter | solution.py:189
  320.2 12.3 %copy-start.31 = (bf16[2,768,768]{2,1,0:T(8,128)(2,1)S(1)}, bf16[2,768,768]{2,1,0:T(8,128)(2,1)}, u32[]{:S(2)}) copy-start(bf16[2,768,768]{2,1,0:T(8,128)(2,1)} %all-gather.16.cloned.1.call-done) | copy-start | bytes 7077892
  330.8 1.7 copy-start.32
  337.0 99.1 %reduce-scatter.11.cloned.1.call-start = ((), (), s32[]{:S(2)}) async-start(), calls=%async_computation.11 | async-start | bytes 3932160 | tf_op jit(solution)/shard_map/reduce_scatter | solution.py:170
  343.6 92.4 %copy-start.29 = (f32[768]{0:T(1024)S(1)}, f32[768]{0:T(1024)}, u32[]{:S(2)}) copy-start(f32[768]{0:T(1024)} %get-tuple-element.525) | copy-start | bytes 9220
  343.7 126.8 %all-gather.20.cloned.1.call-start = ((), (), s32[]{:S(2)}) async-start(), calls=%async_computation.14 | async-start | bytes 3932160 | tf_op jit(solution)/shard_map/all_gather | solution.py:198
  441.8 151.3 %reduce-scatter.15.cloned.1.call-start = ((), (), s32[]{:S(2)}) async-start(), calls=%async_computation.15 | async-start | bytes 3932160 | tf_op jit(solution)/shard_map/reduce_scatter | solution.py:254
  473.5 2.8 copy-start.4
  487.9 1.8 copy-start.16
  490.8 1.6 copy-start.17
  503.9 1.8 copy-start.16
  520.0 1.8 copy-start.16
  522.9 1.7 copy-start.17
  536.1 1.8 copy-start.16
  539.0 1.7 copy-start.17
  540.9 3.8 copy-start.18
  550.8 4.1 copy-start.21
  554.9 111.0 %reduce-scatter.17.cloned.1.call-start = ((), (), s32[]{:S(2)}) async-start(), calls=%async_computation.16 | async-start | bytes 2654208 | tf_op jit(solution)/shard_map/reduce_scatter | solution.py:299
  555.0 5.7 copy-start.30
  555.0 5.7 copy-start.33
  563.4 2.1 copy-start.6
  565.1 167.2 %reduce-scatter.19.cloned.1.call-start = ((), (), s32[]{:S(2)}) async-start(), calls=%async_computation.18 | async-start | bytes 1327104
  565.4 3.0 copy-start.9
  565.4 3.6 copy-start.22
  574.8 18.2 %copy-start.26 = (f32[768]{0:T(1024)S(1)}, f32[768]{0:T(1024)}, u32[]{:S(2)}) copy-start(f32[768]{0:T(1024)} %copy-done.25) | copy-start | bytes 9220
  577.1 19.6 %copy-start.13 = (f32[4,96,192]{2,1,0:T(8,128)S(1)}, f32[4,96,192]{2,1,0:T(8,128)}, u32[]{:S(2)}) copy-start(f32[4,96,192]{2,1,0:T(8,128)} %param.19) | copy-start | bytes 884740
  577.1 212.8 %all-gather.22.cloned.1.call-start = ((), (), s32[]{:S(2)}) async-start(), calls=%async_computation.17 | async-start | bytes 1622016 | tf_op jit(solution)/shard_map/all_gather | solution.py:72
  578.1 87.8 %copy-start.12 = (f32[2,96,768]{2,1,0:T(8,128)S(1)}, f32[2,96,768]{2,1,0:T(8,128)}, u32[]{:S(2)}) copy-start(f32[2,96,768]{2,1,0:T(8,128)} %param.22) | copy-start | bytes 1769476
  578.3 87.6 %copy-start.19 = (f32[2,96,768]{2,1,0:T(8,128)S(1)}, f32[2,96,768]{2,1,0:T(8,128)}, u32[]{:S(2)}) copy-start(f32[2,96,768]{2,1,0:T(8,128)} %param.23) | copy-start | bytes 1769476
  668.6 73.9 %copy-start.2 = (f32[2,256,768]{2,1,0:T(8,128)S(1)}, f32[2,256,768]{2,1,0:T(8,128)}, u32[]{:S(2)}) copy-start(f32[2,256,768]{2,1,0:T(8,128)} %copy-done.1) | copy-start | bytes 4718596
  668.6 73.9 %copy-start.10 = (bf16[2,256,768]{2,1,0:T(8,128)(2,1)S(1)}, bf16[2,256,768]{2,1,0:T(8,128)(2,1)}, u32[]{:S(2)}) copy-start(bf16[2,256,768]{2,1,0:T(8,128)(2,1)} %reduce-scatter.15.cloned.1.call-done) | copy-start | bytes 2359300
  742.5 48.8 %copy-start.24 = (f32[12,768]{1,0:T(8,128)S(1)}, f32[12,768]{1,0:T(8,128)}, u32[]{:S(2)}) copy-start(f32[12,768]{1,0:T(8,128)} %param.25) | copy-start | bytes 110596
  742.5 48.8 %copy-start.27 = (f32[12,768]{1,0:T(8,128)S(1)}, f32[12,768]{1,0:T(8,128)}, u32[]{:S(2)}) copy-start(f32[12,768]{1,0:T(8,128)} %param.26) | copy-start | bytes 110596
  742.5 48.8 %copy-start.28 = (f32[12,768]{1,0:T(8,128)S(1)}, f32[12,768]{1,0:T(8,128)}, u32[]{:S(2)}) copy-start(f32[12,768]{1,0:T(8,128)} %param.27) | copy-start | bytes 110596
  (6 other events, 7.3 us)
Sparse Core Ops, SparseCore 0:
  10.8 46.8 all-gather.11
  59.2 27.3 all-gather.9
  147.8 58.3 reduce-scatter.8
  209.0 51.9 all-gather.15
  263.0 27.0 all-gather.13
  291.6 28.5 all-gather.17
  337.1 58.3 reduce-scatter.12
  398.0 37.9 reduce-scatter.10
  441.9 28.5 all-gather.19
  555.1 37.9 reduce-scatter.14
  596.5 69.3 reduce-scatter.16
  669.2 63.1 reduce-scatter.18
  735.8 54.0 all-gather.21
